TPU v7x, 256 devices: a whole 4x4x8 slice. The times are simulated.
256 devices in a mesh: seq: 64 (over z, x, core), mp: 4 (over y).
Axes of the slice: x: 4, y: 4, z: 8, core: 2. Of those that a mesh axis runs over, the one named last changes fastest.
Arguments:
- span_pairs: bfloat16 [32768, 2, 896], P('seq', None, 'mp'), may hold values from -6 to 6
- dec_queries: bfloat16 [32768, 2048], P('seq', 'mp'), may hold values from -6 to 6
- database: float32 [128, 128, 896], P('seq'), may hold values from -6 to 6
- nbr_index: int32 [512, 2], P('seq'), may hold values from 0 to 1
- nbr_host: int32 [512, 2], P('seq'), may hold values from 0 to 63, as said below
- enc_gain: float32 [896], replicated, may hold values from 0.25 to 1.75
- enc_query: bfloat16 [896, 896], P(None, 'mp'), may hold values from -0.1875 to 0.1875
- enc_out: bfloat16 [896, 896], P('mp'), may hold values from -0.1875 to 0.1875
- ffn_gain: float32 [896], replicated, may hold values from 0.25 to 1.75
- ffn_up: bfloat16 [896, 1792], P(None, 'mp'), may hold values from -0.1875 to 0.1875
- ffn_down: bfloat16 [1792, 896], P('mp'), may hold values from -0.125 to 0.125
- dec_kv: bfloat16 [896, 2, 2048], P(None, None, 'mp'), may hold values from -0.1875 to 0.1875
Outputs:
- attended: float32 [32768, 2048], P('seq', 'mp')
Inputs may be any that keep to these rules, and one draw needn't show every extreme that they name: `nbr_host`: the 16 neighbours of the spans of one seq index name each host at most 1 times, and some host exactly 1 times. Over all spans every host is named exactly 16 times.
All inputs are finite; a program needn't handle non-finite values.
Results may differ from a plain program's by a relative error of at most 0.019.
Values may be sent and summed in bfloat16 or wider, within the bound.
A program may use at most 128 MiB of HBM per device.

v0:
```python
import jax
import jax.numpy as jnp
from jax import lax
from jax.sharding import PartitionSpec as P

HEAD_DIM = 128
EHEAD_DIM = 112
SPAN = 64
NBL = 128
NEIGH = 2
CH_DEV = 8


def split_up(array, dim, length):
    before, after = (array.shape[:dim], array.shape[dim + 1 :])
    return jnp.moveaxis(array.reshape(*before, length, -1, *after), dim, 0)


def sum_at_owner(array, axis, dim):
    tiles = split_up(array, dim, lax.axis_size(axis))
    arrived = lax.all_to_all(tiles, axis, split_axis=0, concat_axis=0, tiled=True)
    return arrived.astype(jnp.float32).sum(axis=0)


def passed_along(array, axis, by):
    length = lax.axis_size(axis)
    pairs = [(i, i + by) for i in range(length) if 0 <= i + by < length]
    return lax.ppermute(array, axis, pairs)


def rms_scale(values, gain):
    return values * lax.rsqrt(jnp.mean(values * values, axis=-1, keepdims=True) + 1e-06) * gain


def on_device(
    span_pairs,
    dec_queries,
    database,
    nbr_index,
    nbr_host,
    enc_gain,
    enc_query,
    enc_out,
    ffn_gain,
    ffn_up,
    ffn_down,
    dec_kv,
):
    seq_size = lax.axis_size("seq")
    lanes = lax.axis_size("mp")
    lane_index = lax.axis_index("mp")
    local_count = NEIGH * CH_DEV
    slot_cap = (local_count + seq_size - 1) // seq_size
    slot_count = seq_size * slot_cap
    width = database.shape[2]
    enc_width = span_pairs.shape[2]
    enc_heads = enc_width // EHEAD_DIM
    enc_scale = float(EHEAD_DIM) ** (-0.5)
    dec_scale = float(HEAD_DIM) ** (-0.5)
    kv_local = span_pairs.reshape(CH_DEV, SPAN, 2, enc_width)
    hosts = nbr_host.reshape(local_count)
    codes = nbr_index.reshape(local_count) + 1
    order = jnp.arange(local_count)
    earlier = (hosts[:, None] == hosts[None, :]) & (order[None, :] < order[:, None])
    ranks = jnp.sum(earlier.astype(jnp.int32), axis=1)
    target = hosts * slot_cap + ranks
    place = jnp.arange(slot_count)[:, None] == target[None, :]
    place_bf = place.astype(jnp.bfloat16).reshape(slot_count, CH_DEV, NEIGH)
    outgoing = jnp.einsum(
        "pmk,mtce->ptce", place_bf, kv_local, preferred_element_type=jnp.float32
    ).astype(jnp.bfloat16)
    out_codes = jnp.sum(place.astype(jnp.int32) * codes[None, :], axis=1)
    incoming, in_codes = (
        lax.all_to_all(
            outgoing.reshape(seq_size, slot_cap, SPAN, 2, enc_width),
            "seq",
            split_axis=0,
            concat_axis=0,
            tiled=True,
        ),
        lax.all_to_all(
            out_codes.reshape(seq_size, slot_cap), "seq", split_axis=0, concat_axis=0, tiled=True
        ),
    )
    in_codes = in_codes.reshape(slot_count)
    live = in_codes > 0
    slot_rank = jnp.cumsum(live.astype(jnp.int32)) - 1
    pick = live[None, :] & (slot_rank[None, :] == jnp.arange(local_count)[:, None])
    pick_bf = pick.astype(jnp.bfloat16)
    packed_kv = jnp.einsum(
        "ap,ptce->atce",
        pick_bf,
        incoming.reshape(slot_count, SPAN, 2, enc_width),
        preferred_element_type=jnp.float32,
    ).astype(jnp.bfloat16)
    packed_codes = jnp.sum(pick.astype(jnp.int32) * in_codes[None, :], axis=1)
    packed_entry = jnp.maximum(packed_codes - 1, 0)
    neighbours = jnp.swapaxes(jnp.take(database, packed_entry, axis=0), 0, 1)
    normed = rms_scale(neighbours, enc_gain).astype(jnp.bfloat16)
    query = (
        jnp.einsum("rae,ef->raf", normed, enc_query, preferred_element_type=jnp.float32) * enc_scale
    ).astype(jnp.bfloat16)
    query = query.reshape(NBL, local_count, enc_heads, EHEAD_DIM)
    keys = packed_kv[:, :, 0].reshape(local_count, SPAN, enc_heads, EHEAD_DIM)
    values = packed_kv[:, :, 1].reshape(local_count, SPAN, enc_heads, EHEAD_DIM)
    scores = jnp.einsum("rahd,akhd->ahrk", query, keys, preferred_element_type=jnp.float32)
    weights = jax.nn.softmax(scores, axis=-1).astype(jnp.bfloat16)
    enc_attended = jnp.einsum(
        "ahrk,akhd->rahd", weights, values, preferred_element_type=jnp.float32
    )
    enc_attended = enc_attended.astype(jnp.bfloat16).reshape(NBL, local_count, enc_width)
    partial_value = jnp.einsum(
        "raf,fe->rae", enc_attended, enc_out, preferred_element_type=jnp.float32
    )
    row_count = NBL // lanes
    row_start = lane_index * row_count
    mixed = sum_at_owner(partial_value.astype(jnp.bfloat16), "mp", 0)
    resid = lax.dynamic_slice_in_dim(neighbours, row_start, row_count, 0) + mixed
    up_full, down_full = (
        lax.all_gather(ffn_up, "mp", axis=1, tiled=True),
        lax.all_gather(ffn_down, "mp", axis=0, tiled=True),
    )
    unit_width = ffn_up.shape[1]
    inner = rms_scale(resid, ffn_gain).astype(jnp.bfloat16)
    units = jax.nn.gelu(
        jnp.einsum("rae,ef->raf", inner, up_full, preferred_element_type=jnp.float32)
    ).astype(jnp.bfloat16)
    units = units.reshape(row_count, local_count, lanes, unit_width)
    down_terms = jnp.einsum(
        "ragf,gfe->rage",
        units,
        down_full.reshape(lanes, unit_width, width),
        preferred_element_type=jnp.float32,
    )
    down_terms = down_terms.astype(jnp.bfloat16).astype(jnp.float32)
    encoded = (resid + jnp.sum(down_terms, axis=2)).astype(jnp.bfloat16)
    returning = jnp.einsum(
        "ap,rae->pre", pick_bf, encoded, preferred_element_type=jnp.float32
    ).astype(jnp.bfloat16)
    answers = lax.all_to_all(
        returning.reshape(seq_size, slot_cap, row_count, width),
        "seq",
        split_axis=0,
        concat_axis=0,
        tiled=True,
    )
    mine = jnp.einsum(
        "pmk,pre->mkre",
        place_bf,
        answers.reshape(slot_count, row_count, width),
        preferred_element_type=jnp.float32,
    ).astype(jnp.bfloat16)
    previous = passed_along(mine[CH_DEV - 1], "seq", 1)
    used = jnp.concatenate([previous[None], mine[: CH_DEV - 1]], axis=0)
    dec_width = dec_kv.shape[2]
    dec_heads = dec_width // HEAD_DIM
    dec_pairs = jnp.einsum(
        "mkre,ecd->mkrcd",
        lax.all_gather(used, "mp", axis=2, tiled=True),
        dec_kv,
        preferred_element_type=jnp.float32,
    ).astype(jnp.bfloat16)
    dec_keys = dec_pairs[:, :, :, 0].reshape(CH_DEV, NEIGH * NBL, dec_heads, HEAD_DIM)
    dec_values = dec_pairs[:, :, :, 1].reshape(CH_DEV, NEIGH * NBL, dec_heads, HEAD_DIM)
    dec_q = (dec_queries.astype(jnp.float32) * dec_scale).astype(jnp.bfloat16)
    dec_q = dec_q.reshape(CH_DEV, SPAN, dec_heads, HEAD_DIM)
    dec_scores = jnp.einsum("mqhd,mkhd->mhqk", dec_q, dec_keys, preferred_element_type=jnp.float32)
    dec_weights = jax.nn.softmax(dec_scores, axis=-1).astype(jnp.bfloat16)
    result = jnp.einsum(
        "mhqk,mkhd->mqhd", dec_weights, dec_values, preferred_element_type=jnp.float32
    )
    return result.reshape(CH_DEV * SPAN, dec_width)


def solution(mesh):
    placed = (
        P("seq", None, "mp"),
        P("seq", "mp"),
        P("seq", None, None),
        P("seq", None),
        P("seq", None),
        P(),
        P(None, "mp"),
        P("mp", None),
        P(),
        P(None, "mp"),
        P("mp", None),
        P(None, None, "mp"),
    )
    return jax.shard_map(
        on_device, mesh=mesh, in_specs=placed, out_specs=P("seq", "mp"), check_vma=False
    )
```

profile of v0, /device:TPU:1, one launch (start us, length us, event | category | flops | bytes accessed | tf_op | source)
XLA Modules:
  0.0 409.3 jit_solution(15261873891261934162)
XLA Ops:
  9.4 13.0 %all-to-all-start = ((s32[64,1,1]{2,1,0:T(1,128)}), s32[64,1,1]{2,1,0:T(1,128)S(1)}, u32[]{:S(2)}, u32[]{:S(2)}) async-start(s32[64,1,1]{2,1,0:T(1,128)} %copy.120), calls=%async_computation | async-start | bytes 65536 | tf_op jit(solution)/shard_map/all_to_all | solution.py:81
  25.8 6.4 %copy.125 = bf16[64,1,64,2,224]{4,3,2,1,0:T(2,128)(2,1)} copy(bf16[64,1,64,2,224]{4,0,3,2,1:T(8,128)(2,1)S(1)} %convert_bitcast_fusion) | data formatting | bytes 7340032 | tf_op jit(solution)/shard_map/reshape | solution.py:75
  32.2 10.6 %all-to-all-start.1 = ((bf16[64,1,64,2,224]{4,3,2,1,0:T(2,128)(2,1)}), bf16[64,1,64,2,224]{4,3,2,1,0:T(2,128)(2,1)}, u32[]{:S(2)}, u32[]{:S(2)}) async-start(bf16[64,1,64,2,224]{4,3,2,1,0:T(2,128)(2,1)} %copy.125), calls=%async_computation.1 | async-start | bytes 8388608 | tf_op jit(solution)/shard_map/all_to_all | solution.py:74
  45.2 4.0 gather_fusion
  49.2 4.1 fusion.2
  53.3 2.9 copy-done.2
  57.8 79.7 %all-to-all-done.1 = bf16[64,1,64,2,224]{4,3,2,1,0:T(2,128)(2,1)} async-done(((bf16[64,1,64,2,224]{4,3,2,1,0:T(2,128)(2,1)}), bf16[64,1,64,2,224]{4,3,2,1,0:T(2,128)(2,1)}, u32[]{:S(2)}, u32[]{:S(2)}) %all-to-all-start.1) | async-done | bytes 3670048 | tf_op jit(solution)/shard_map/all_to_all | solution.py:74
  137.5 4.5 %fusion.39 = bf16[16,64,2,224]{3,0,2,1:T(8,128)(2,1)S(1)} fusion(bf16[64,1,64,2,224]{4,3,2,1,0:T(2,128)(2,1)} %all-to-all-done.1, s32[64]{0:T(128)S(1)} %add_reduce_fusion, pred[64]{0:T(512)(128)(4,1)S(1)} %broadcast_compare_fusion.1), kind=kOutput, calls=%fused_computation.51 | convolution fusion | flops 59181056 | bytes 4587840 | tf_op jit(solution)/shard_map/ap,ptce->atce/dot_general | solution.py:90
  147.0 2.3 convolution_convert_fusion.1
  152.9 4.7 %all-to-all-start.2 = ((bf16[4,32,16,896]{3,1,2,0:T(8,128)(2,1)}), bf16[4,32,16,896]{3,1,2,0:T(8,128)(2,1)}, u32[]{:S(2)}, u32[]{:S(2)}) async-start(bf16[4,32,16,896]{3,1,2,0:T(8,128)(2,1)} %copy.129), calls=%async_computation.2 | async-start | bytes 7340032 | tf_op jit(solution)/shard_map/all_to_all | solution.py:21
  157.9 41.0 %all-to-all-done.2 = bf16[4,32,16,896]{3,1,2,0:T(8,128)(2,1)} async-done(((bf16[4,32,16,896]{3,1,2,0:T(8,128)(2,1)}), bf16[4,32,16,896]{3,1,2,0:T(8,128)(2,1)}, u32[]{:S(2)}, u32[]{:S(2)}) %all-to-all-start.2) | async-done | bytes 3670048 | tf_op jit(solution)/shard_map/all_to_all | solution.py:21
  198.9 2.7 convert_reduce_fusion.1
  204.9 5.8 %fusion.15 = bf16[32,16,1792]{2,1,0:T(8,128)(2,1)} fusion(bf16[896,1792]{0,1:T(8,128)(2,1)} %all-gather.4.cloned.1.call-done, bf16[32,16,896]{2,0,1:T(8,128)(2,1)S(1)} %multiply_convert_fusion), kind=kOutput, calls=%fused_computation.22 | convolution fusion | flops 1652424704 | bytes 5963776 | tf_op jit(solution)/shard_map/rae,ef->raf/dot_general | solution.py:126
  210.8 6.2 %reshape.188 = bf16[32,16,4,448]{3,2,1,0:T(4,128)(2,1)} reshape(bf16[32,16,1792]{2,1,0:T(8,128)(2,1)} %fusion.15) | data formatting | bytes 3670016 | tf_op jit(solution)/shard_map/reshape | solution.py:128
  216.9 5.1 %convert_reduce_fusion = f32[32,16,896]{2,1,0:T(8,128)S(1)} fusion(bf16[4,448,896,1]{2,1,3,0:T(8,128)(2,1)} %bitcast.122, bf16[32,16,4,448]{3,2,1,0:T(4,128)(2,1)} %reshape.188), kind=kOutput, calls=%fused_computation.8 | convolution fusion | flops 1649213440 | bytes 6881280 | tf_op jit(solution)/shard_map/ragf,gfe->rage/dot_general | solution.py:129
  226.0 93.1 %all_to_all.24 = bf16[64,1,32,896]{3,2,1,0:T(8,128)(2,1)S(1)} all-to-all(bf16[64,1,32,896]{3,2,1,0:T(8,128)(2,1)S(1)} %copy.134), channel_id=1, replica_groups=mesh['seq'=64,'mp'=4] {'seq'}, dimensions={0} | all-to-all | bytes 7340032 | tf_op jit(solution)/shard_map/all_to_all | solution.py:140
  321.2 4.3 %collective-permute-start = (bf16[2,32,896]{2,1,0:T(8,128)(2,1)S(1)}, bf16[2,32,896]{2,1,0:T(8,128)(2,1)S(1)}, u32[]{:S(2)}, u32[]{:S(2)}) collective-permute-start(bf16[2,32,896]{2,1,0:T(8,128)(2,1)S(1)} %bitcast.118), channel_id=1, source_target_pairs={{0,4},{4,8},{8,12},{12,16},{16,20},{20,24},{24,28},{28,32},{32,36}... | collective-permute-start | bytes 344072 | tf_op jit(solution)/shard_map/ppermute | solution.py:28
  329.1 43.4 %all-gather.8.cloned.1.call-done = bf16[8,2,128,896]{3,0,2,1:T(8,128)(2,1)} async-done(((bf16[8,2,32,896]{3,0,2,1:T(8,128)(2,1)}), bf16[8,2,128,896]{3,0,2,1:T(8,128)(2,1)}) %all-gather.8.cloned.1.call-update) | async-done | bytes 3670032 | tf_op jit(solution)/shard_map/all_gather | solution.py:159
  372.5 6.8 %fusion.29 = bf16[8,2,128,2,512]{4,2,3,1,0:T(8,128)(2,1)S(1)} fusion(bf16[8,2,128,896,1]{3,0,2,1,4:T(8,128)(2,1)} %bitcast.121, bf16[896,2,512,1,1]{2,1,0,4,3:T(2,128)(2,1)S(1)} %bitcast.110), kind=kOutput, calls=%fused_computation.35 | convolution fusion | flops 3760193536 | bytes 9699328 | tf_op jit(solution)/shard_map/mkre,ecd->mkrcd/dot_general | solution.py:157
  379.3 2.5 fusion.80
  381.8 4.0 reshape_squeeze.14
  385.7 4.0 reshape_squeeze.15
  389.7 2.4 fusion.34
  394.1 6.5 %fusion.49 = f32[8,64,4,128]{3,1,2,0:T(8,128)S(1)} fusion(bf16[8,256,4,128]{3,2,1,0:T(4,128)(2,1)} %reshape_squeeze.14, f32[8,4,64]{2,1,0:T(4,128)S(1)} %fusion.83, f32[8,4,64,256]{3,2,1,0:T(8,128)} %copy-done.5), kind=kOutput, calls=%fused_computation.56 | convolution fusion | flops 135792896 | bytes 5251072 | tf_op jit(solution)/shard_map/mhqk,mkhd->mqhd/dot_general | solution.py:169
  (82 shorter events, 35.3 us)
Async XLA Ops:
  6.5 366.0 %copy-start = (bf16[896,2,512]{2,1,0:T(2,128)(2,1)S(1)}, bf16[896,2,512]{2,1,0:T(2,128)(2,1)}, u32[]{:S(2)}) copy-start(bf16[896,2,512]{2,1,0:T(2,128)(2,1)} %param.23) | copy-start | bytes 5505028
  9.4 22.9 %all-to-all-start = ((s32[64,1,1]{2,1,0:T(1,128)}), s32[64,1,1]{2,1,0:T(1,128)S(1)}, u32[]{:S(2)}, u32[]{:S(2)}) async-start(s32[64,1,1]{2,1,0:T(1,128)} %copy.120), calls=%async_computation | async-start | bytes 65536 | tf_op jit(solution)/shard_map/all_to_all | solution.py:81
  22.3 182.6 %all-gather.4.cloned.1.call-start = ((), (), s32[]{:S(2)}) async-start(), calls=%async_computation.4 | async-start | bytes 4014080 | tf_op jit(solution)/shard_map/all_gather | solution.py:120
  32.2 13.0 %copy-start.1 = (f32[2,128,896]{2,1,0:T(8,128)S(1)}, f32[2,128,896]{2,1,0:T(8,128)}, u32[]{:S(2)}) copy-start(f32[2,128,896]{2,1,0:T(8,128)} %param.14) | copy-start | bytes 2752516
  32.2 105.3 %all-to-all-start.1 = ((bf16[64,1,64,2,224]{4,3,2,1,0:T(2,128)(2,1)}), bf16[64,1,64,2,224]{4,3,2,1,0:T(2,128)(2,1)}, u32[]{:S(2)}, u32[]{:S(2)}) async-start(bf16[64,1,64,2,224]{4,3,2,1,0:T(2,128)(2,1)} %copy.125), calls=%async_computation.1 | async-start | bytes 8388608 | tf_op jit(solution)/shard_map/all_to_all | solution.py:74
  42.8 174.1 %all-gather.6.cloned.1.call-start = ((), (), s32[]{:S(2)}) async-start(), calls=%async_computation.5 | async-start | bytes 4014080 | tf_op jit(solution)/shard_map/all_gather | solution.py:121
  49.2 7.1 %copy-start.9 = (bf16[896,224]{0,1:T(8,128)(2,1)S(1)}, bf16[896,224]{0,1:T(8,128)(2,1)}, u32[]{:S(2)}) copy-start(bf16[896,224]{0,1:T(8,128)(2,1)} %param.18) | copy-start | bytes 1204228
  49.2 7.1 %copy-start.10 = (f32[896]{0:T(1024)S(1)}, f32[896]{0:T(1024)}, u32[]{:S(2)}) copy-start(f32[896]{0:T(1024)} %param.17) | copy-start | bytes 10756
  53.3 3.0 copy-start.2
  145.7 1.0 copy-start.6
  146.7 2.6 copy-start.8
  152.9 46.0 %all-to-all-start.2 = ((bf16[4,32,16,896]{3,1,2,0:T(8,128)(2,1)}), bf16[4,32,16,896]{3,1,2,0:T(8,128)(2,1)}, u32[]{:S(2)}, u32[]{:S(2)}) async-start(bf16[4,32,16,896]{3,1,2,0:T(8,128)(2,1)} %copy.129), calls=%async_computation.2 | async-start | bytes 7340032 | tf_op jit(solution)/shard_map/all_to_all | solution.py:21
  157.6 214.9 %all-gather.8.cloned.1.call-start = ((), (), s32[]{:S(2)}) async-start(), calls=%async_computation.6 | async-start | bytes 4587520 | tf_op jit(solution)/shard_map/all_gather | solution.py:159
  201.6 3.0 copy-start.11
  203.4 1.2 copy-start.3
  216.9 5.1 %copy-start.4 = (f32[32,16,896]{2,0,1:T(8,128)S(1)}, f32[32,16,896]{2,0,1:T(8,128)}, u32[]{:S(2)}) copy-start(f32[32,16,896]{2,0,1:T(8,128)} %copy-done.3) | copy-start | bytes 5505028
  320.9 8.0 %copy-start.7 = (bf16[512,512]{1,0:T(8,128)(2,1)S(1)}, bf16[512,512]{1,0:T(8,128)(2,1)}, u32[]{:S(2)}) copy-start(bf16[512,512]{1,0:T(8,128)(2,1)} %param.13) | copy-start | bytes 1572868
  321.2 6.1 %collective-permute-start = (bf16[2,32,896]{2,1,0:T(8,128)(2,1)S(1)}, bf16[2,32,896]{2,1,0:T(8,128)(2,1)S(1)}, u32[]{:S(2)}, u32[]{:S(2)}) collective-permute-start(bf16[2,32,896]{2,1,0:T(8,128)(2,1)S(1)} %bitcast.118), channel_id=1, source_target_pairs={{0,4},{4,8},{8,12},{12,16},{16,20},{20,24},{24,28},{28,32},{32,36}... | collective-permute-start | bytes 344072 | tf_op jit(solution)/shard_map/ppermute | solution.py:28
  392.1 1.3 copy-start.5
Sparse Core Ops, SparseCore 0:
  25.0 43.5 all-gather.3
  70.3 42.7 all-gather.5
  329.0 43.4 all-gather.7
where the time goes:
time: 416 us; the launch traced here: 409 us
  waiting for transfers between devices  167 us (40%)
  blocking collectives  93.1 us (22%)
  local copies, waits for them, and re-layouts  46.6 us (11%)
  matrix products  41 us (10%)
  starting transfers between devices  33.1 us (8%)
  other arithmetic  14.5 us (3%)
  between operations  13.9 us (3%)
    all_to_all x1, blocking collectives, on_device(): lax.all_to_all(returning.reshape(seq_size, slot_cap, row_count, width), '...  93.1 us
    all_to_all x1, waiting for transfers between devices, on_device(): lax.all_to_all(outgoing.reshape(seq_size, slot_cap, SPAN, 2, enc_width),...  79.7 us
    all_gather x1, waiting for transfers between devices, on_device(): lax.all_gather(used, 'mp', axis=2, tiled=True)  43.4 us
    all_to_all x1, waiting for transfers between devices, sum_at_owner(): lax.all_to_all(tiles, axis, split_axis=0, concat_axis=0, tiled=True)  41 us
    all_to_all x1, starting transfers between devices, on_device(): lax.all_to_all(out_codes.reshape(seq_size, slot_cap), 'seq', split_axis=0...  13 us
    all_to_all x1, starting transfers between devices, on_device(): lax.all_to_all(outgoing.reshape(seq_size, slot_cap, SPAN, 2, enc_width),...  10.6 us
    unnamed x28, local copies, waits for them, and re-layouts  9.63 us
  transfers between devices with their start and end apart: 7, of which 4 were waited for; matrix products, arithmetic and copies ran while one was open for 13% of the time, Pallas kernels for 0%

commit v1 on v0

v1 whole, which is shorter than its diff:
```python
import jax
import jax.numpy as jnp
from jax import lax
from jax.experimental import pallas as pl
from jax.experimental.pallas import tpu as pltpu
from jax.sharding import PartitionSpec as P

HEAD_DIM = 128
EHEAD_DIM = 112
SPAN = 64
NBL = 128
NEIGH = 2
CH_DEV = 8
NZ, NX, NC, NY = 8, 4, 2, 4
E = 896
LANE = 224
UNIT = 448
DLANE = 512
QROWS = NBL // NY
ROWS = 2 * NEIGH * NBL
F32 = jnp.float32
BF16 = jnp.bfloat16
MESH_ID = pl.DeviceIdType.MESH
SEMS = 160


def rms_scale(values, gain):
    return values * lax.rsqrt(jnp.mean(values * values, axis=-1, keepdims=True) + 1e-06) * gain


class Net:
    def __init__(self, send_sem, recv_sem, copy_sem, any_dev):
        self.send_sem, self.recv_sem, self.copy_sem = send_sem, recv_sem, copy_sem
        self.any_dev = any_dev
        self.count = 0
        self.local_count = 0
        self.sent = []

    def number(self, many=1):
        first = self.count
        self.count += many
        return first

    def describe(self, src, dst, i, dev, j=None):
        return pltpu.make_async_remote_copy(
            src_ref=src,
            dst_ref=dst,
            send_sem=self.send_sem.at[i],
            recv_sem=self.recv_sem.at[i if j is None else j],
            device_id=dev,
            device_id_type=MESH_ID,
        )

    def send(self, src, dst, dev):
        i = self.number()
        copy = self.describe(src, dst, i, dev)
        copy.start()
        self.sent.append(copy)
        return i

    def recv(self, i, view):
        self.describe(view, view, i, self.any_dev).wait_recv()

    def local(self, src, dst):
        copy = pltpu.make_async_copy(src, dst, self.copy_sem.at[self.local_count])
        self.local_count += 1
        copy.start()
        return copy


class Ring:
    def __init__(self, net, n, p, right, left, views, halves):
        self.net, self.n, self.p = net, n, p
        self.right, self.left = right, left
        self.views, self.halves = views, halves
        self.numbers = None

    def first(self, sources=None):
        self.numbers = []
        for a, view in enumerate(self.views):
            own = view(self.p, slice(None))
            src = own if sources is None else sources[a]
            self.numbers.append((self.net.send(src, own, self.right), self.net.send(src, own, self.left)))

    def arrive(self, k):
        n, p = self.n, self.p
        before, after = lax.rem(p + n - k, n), lax.rem(p + k, n)
        last = k == n // 2
        numbers = []
        for a, view in enumerate(self.views):
            from_left, from_right = self.numbers[a]
            lo, hi = self.halves[a]
            self.net.recv(from_left, view(before, lo if last else slice(None)))
            self.net.recv(from_right, view(after, hi if last else slice(None)))
            if last:
                continue
            half = k + 1 == n // 2
            left_block = view(before, lo if half else slice(None))
            right_block = view(after, hi if half else slice(None))
            numbers.append(
                (
                    self.net.send(left_block, left_block, self.right),
                    self.net.send(right_block, right_block, self.left),
                )
            )
        self.numbers = numbers
        return before, after


def cut(rows, at):
    return pl.ds(0, at), pl.ds(at, rows - at)


def kernel(
    host_ref,
    index_ref,
    db_hbm,
    kv_hbm,
    q_hbm,
    wq_hbm,
    wo_hbm,
    up_hbm,
    dn_hbm,
    wb_hbm,
    gain_a,
    gain_b,
    out_ref,
    DB,
    WQ,
    WO,
    UP,
    DN,
    WB,
    KV,
    Q,
    SEL,
    EN,
    OUTB,
    NORM,
    ACC,
    ORECV,
    send_sem,
    recv_sem,
    copy_sem,
):
    seq = lax.axis_index("seq")
    y = lax.axis_index("mp")
    z, x, c = seq // (NX * NC), lax.rem(seq // NC, NX), lax.rem(seq, NC)

    def at(zz, xx, cc, yy):
        return ((zz * NX + xx) * NC + cc, yy)

    def lane(d):
        return lax.rem(y + d, NY)

    x_right, x_left = at(z, lax.rem(x + 1, NX), c, y), at(z, lax.rem(x + NX - 1, NX), c, y)
    z_right, z_left = at(lax.rem(z + 1, NZ), x, c, y), at(lax.rem(z + NZ - 1, NZ), x, c, y)
    y_right, y_left, y_far = (seq, lane(1)), (seq, lane(3)), (seq, lane(2))
    partner = at(z, x, 1 - c, y)
    seq_next, seq_prev = lax.rem(seq + 1, NZ * NX * NC), lax.rem(seq + NZ * NX * NC - 1, NZ * NX * NC)
    follow = (seq_next, 0)

    barrier = pltpu.get_barrier_semaphore()

    def greet(dev):
        pl.semaphore_signal(barrier, inc=1, device_id=dev, device_id_type=MESH_ID)

    for dev in (x_right, x_left, z_right, z_left, y_right, y_left, y_far, partner, follow):
        greet(dev)

    @pl.when(y == 0)
    def _():
        for g in range(NY):
            greet((seq_prev, g))
        pl.semaphore_wait(barrier, 8 + 1 + NY)

    @pl.when(y != 0)
    def _():
        pl.semaphore_wait(barrier, 8 + 1)

    net = Net(send_sem, recv_sem, copy_sem, partner)
    half16 = cut(32, 16)
    whole = slice(None)

    one_x = Ring(net, NX, x, x_right, x_left, [lambda p, r: DB.at[z, p, c, 0, r, :]], [half16])
    one_z = Ring(net, NZ, z, z_right, z_left, [lambda p, r: DB.at[p, :, c, 0, r, :]], [half16])
    two_z = Ring(net, NZ, z, z_right, z_left, [lambda p, r: DB.at[p, x, c, 1, r, :]], [half16])
    two_x = Ring(net, NX, x, x_right, x_left, [lambda p, r: DB.at[:, p, c, 1, r, :]], [half16])
    one_x.first([db_hbm.at[0]])
    two_z.first([db_hbm.at[1]])
    db_own = net.local(db_hbm, DB.at[z, x, c])

    early = []

    def to_lanes(src_two, src_one, dst_two, dst_one):
        first = net.number(3)
        for d in range(1, NY):
            dest, slot, i = lane(d), NY - d, first + d - 1

            @pl.when(dest != 0)
            def _():
                net.describe(src_two(2 * dest - 1), dst_two(slot), i, (seq, dest)).start()

            @pl.when(dest == 0)
            def _():
                net.describe(src_one(0), dst_one(slot, 1), i, (seq, dest)).start()

        tail = net.number(NY)
        net.describe(src_one(CH_DEV - 1), dst_one(y, 0), tail, follow, tail + y).start()
        return first, tail

    def lanes_arrived(first, tail, dst_two, dst_one):
        for d in range(1, NY):
            slot, i = NY - d, first + d - 1

            @pl.when(y != 0)
            def _():
                net.recv(i, dst_two(slot))

            @pl.when(y == 0)
            def _():
                net.recv(i, dst_one(slot, 1))

        @pl.when(y == 0)
        def _():
            for g in range(NY):
                net.recv(tail + g, dst_one(g, 0))

    def lanes_sent(first, tail, src_two, src_one):
        for d in range(1, NY):
            dest, i = lane(d), first + d - 1

            @pl.when(dest != 0)
            def _():
                net.describe(src_two(0), src_two(0), i, partner).wait_send()

            @pl.when(dest == 0)
            def _():
                net.describe(src_one(0), src_one(0), i, partner).wait_send()

        net.describe(src_one(0), src_one(0), tail, partner).wait_send()

    kv_src_two = lambda m: kv_hbm.at[:, pl.ds(m, 2)]
    kv_src_one = lambda m: kv_hbm.at[:, pl.ds(m, 1)]
    kv_dst_two = lambda slot: KV.at[slot]
    kv_dst_one = lambda slot, pos: KV.at[slot, :, pl.ds(pos, 1)]
    kv_numbers = to_lanes(kv_src_two, kv_src_one, kv_dst_two, kv_dst_one)
    kv_own = net.local(kv_hbm.at[:, pl.ds(2 * y, 1)], KV.at[0, :, pl.ds(1, 1)])

    @pl.when(y != 0)
    def _():
        pltpu.make_async_copy(
            kv_hbm.at[:, pl.ds(2 * y - 1, 1)], KV.at[0, :, pl.ds(0, 1)], copy_sem.at[40]
        ).start()

    piece = 2 * x + c
    low_piece = jnp.minimum(piece, 6)
    halves_a = [cut(112, 64), cut(32, 16), cut(112, 64), cut(64, 32)]
    bufs_a = [WQ, WO, UP, DN]
    srcs_a = [wq_hbm.at[x, c], wo_hbm.at[low_piece], up_hbm.at[x, c], dn_hbm.at[low_piece]]

    def y_first(buf, src, i, j):
        return net.send(src, buf.at[3, i, j], y_right), net.send(src, buf.at[1, i, j], y_left)

    def y_relay(buf, halves, numbers, i, j):
        lo, hi = halves
        net.recv(numbers[0], buf.at[3, i, j])
        a = net.send(buf.at[3, i, j, lo, :], buf.at[2, i, j, lo, :], y_right)
        net.recv(numbers[1], buf.at[1, i, j])
        b = net.send(buf.at[1, i, j, hi, :], buf.at[2, i, j, hi, :], y_left)
        return a, b

    def y_last(buf, halves, numbers, i, j):
        lo, hi = halves
        net.recv(numbers[0], buf.at[2, i, j, lo, :])
        net.recv(numbers[1], buf.at[2, i, j, hi, :])

    ya = [y_first(bufs_a[a], srcs_a[a], x, c) for a in range(4)]
    q_numbers = []
    for d in range(1, NY):
        q_numbers.append(
            net.send(q_hbm.at[pl.ds(lane(d) * 128, 128)], Q.at[NY - d], (seq, lane(d)))
        )
    yb = y_first(WB, wb_hbm.at[z, c], z, c)
    own = [
        net.local(wq_hbm, WQ.at[0]),
        net.local(up_hbm, UP.at[0]),
        net.local(wb_hbm, WB.at[0]),
        net.local(q_hbm.at[pl.ds(y * 128, 128)], Q.at[0]),
    ]
    for i in range(7):
        own.append(net.local(wo_hbm.at[i], WO.at[0, i // 2, i % 2]))
        own.append(net.local(dn_hbm.at[i], DN.at[0, i // 2, i % 2]))

    others = pl.ds(1, 3)

    def view_a(buf):
        return lambda p, r: buf.at[others, p, c, r, :]

    ring_qo = Ring(net, NX, x, x_right, x_left, [view_a(WQ), view_a(WO)], halves_a[:2])
    ring_ud = Ring(net, NX, x, x_right, x_left, [view_a(UP), view_a(DN)], halves_a[2:])
    ring_b = Ring(net, NZ, z, z_right, z_left, [view_a(WB)], [cut(112, 64)])

    across = []

    def share(view):
        across.append((net.send(view(c), view(c), partner), view))

    def shared_here(items):
        for i, view in items:
            net.recv(i, view(1 - c))

    one_x.arrive(1)
    two_z.arrive(1)
    db_own.wait()
    one_x.arrive(2)
    one_z.first()
    share(lambda s: DB.at[z, :, s, 0])
    two_z.arrive(2)
    two_z.arrive(3)
    ya[0] = y_relay(WQ, halves_a[0], ya[0], x, c)
    ya[1] = y_relay(WO, halves_a[1], ya[1], x, c)
    two_z.arrive(4)
    two_x.first()
    share(lambda s: DB.at[:, x, s, 1])

    def one_step(k):
        before, after = one_z.arrive(k)
        share(lambda s: DB.at[before, :, s, 0])
        if k < NZ // 2:
            share(lambda s: DB.at[after, :, s, 0])

    def two_step(k):
        before, after = two_x.arrive(k)
        share(lambda s: DB.at[:, before, s, 1])
        if k < NX // 2:
            share(lambda s: DB.at[:, after, s, 1])

    y_last(WQ, halves_a[0], ya[0], x, c)
    y_last(WO, halves_a[1], ya[1], x, c)
    ring_qo.first()
    one_step(1)
    ya[2] = y_relay(UP, halves_a[2], ya[2], x, c)
    ya[3] = y_relay(DN, halves_a[3], ya[3], x, c)
    one_step(2)
    two_step(1)
    yb = y_relay(WB, cut(112, 64), yb, z, c)
    y_last(UP, halves_a[2], ya[2], x, c)
    y_last(DN, halves_a[3], ya[3], x, c)
    ring_ud.first()
    one_step(3)
    y_last(WB, cut(112, 64), yb, z, c)
    ring_b.first()
    ring_qo.arrive(1)
    two_step(2)
    one_step(4)
    shared_here(across)
    db_across = len(across)

    for m in range(CH_DEV):
        for k in range(NEIGH):
            host = host_ref[m, k]
            SEL[m, k] = DB[host // (NX * NC), lax.rem(host // NC, NX), lax.rem(host, NC), index_ref[m, k]]
    e_src_two = lambda m: SEL.at[pl.ds(m, 2)]
    e_src_one = lambda m: SEL.at[pl.ds(m, 1)]
    e_dst_two = lambda slot: EN.at[:, slot]
    e_dst_one = lambda slot, pos: EN.at[pl.ds(pos, 1), slot]
    e_numbers = to_lanes(e_src_two, e_src_one, e_dst_two, e_dst_one)
    EN[1, 0] = SEL[2 * y]

    @pl.when(y != 0)
    def _():
        EN[0, 0] = SEL[2 * y - 1]

    ring_qo.arrive(2)
    share(lambda s: WQ.at[others, :, s])
    share(lambda s: WO.at[others, :, s])
    ring_ud.arrive(1)
    ring_b.arrive(1)
    lanes_arrived(*kv_numbers, kv_dst_two, kv_dst_one)
    kv_own.wait()

    @pl.when(y != 0)
    def _():
        pltpu.make_async_copy(
            kv_hbm.at[:, pl.ds(2 * y - 1, 1)], KV.at[0, :, pl.ds(0, 1)], copy_sem.at[40]
        ).wait()

    for copy in own:
        copy.wait()
    for d in range(1, NY):
        net.recv(q_numbers[d - 1], Q.at[NY - d])
    lanes_arrived(*e_numbers, e_dst_two, e_dst_one)

    neighbours = EN[...].reshape(ROWS, E).astype(F32)
    ACC[...] = neighbours
    NORM[...] = rms_scale(neighbours, gain_a[...]).astype(BF16)
    shared_here(across[db_across:])

    head_of_row = lax.broadcasted_iota(jnp.int32, (2 * SPAN, LANE), 0) >= SPAN
    head_of_lane = lax.broadcasted_iota(jnp.int32, (2 * SPAN, LANE), 1) >= EHEAD_DIM
    head_mask = jnp.where(head_of_row == head_of_lane, 1.0, 0.0).astype(BF16)
    last_last = (((1,), (1,)), ((), ()))
    first_first = (((0,), (0,)), ((), ()))

    def attend(k, carry):
        query = jnp.dot(NORM[...], WQ[k].reshape(E, LANE), preferred_element_type=F32)
        query = (query * float(EHEAD_DIM) ** -0.5).astype(BF16)
        w_out = WO[k].reshape(256, E)[:LANE]
        for pos in range(2):
            keys = KV[k, 0, pos]
            values = KV[k, 1, pos]
            keys = jnp.concatenate([keys, keys], axis=0) * head_mask
            values = jnp.concatenate([values, values], axis=0) * head_mask
            mine = query[pos * 256 : (pos + 1) * 256]
            scores = lax.dot_general(keys, mine, last_last, preferred_element_type=F32)
            scores = scores.reshape(2, SPAN, 256)
            top = jnp.max(scores, axis=1, keepdims=True)
            parts = jnp.exp(scores - top)
            parts = parts / jnp.sum(parts, axis=1, keepdims=True)
            weights = parts.reshape(2 * SPAN, 256).astype(BF16)
            got = lax.dot_general(weights, values, first_first, preferred_element_type=F32)
            ACC[pl.ds(pos * 256, 256), :] += jnp.dot(
                got.astype(BF16), w_out, preferred_element_type=F32
            )
        return carry

    lax.fori_loop(0, NY, attend, 0)
    ring_ud.arrive(2)
    ud = len(across)
    share(lambda s: UP.at[others, :, s])
    share(lambda s: DN.at[others, :, s])
    ring_b.arrive(2)
    NORM[...] = rms_scale(ACC[...], gain_b[...]).astype(BF16)
    shared_here(across[ud:])

    def feed(k, carry):
        units = jnp.dot(NORM[...], UP[k].reshape(E, UNIT), preferred_element_type=F32)
        units = jax.nn.gelu(units).astype(BF16)
        ACC[...] += jnp.dot(units, DN[k].reshape(512, E)[:UNIT], preferred_element_type=F32)
        return carry

    lax.fori_loop(0, 2, feed, 0)
    ring_b.arrive(3)
    lax.fori_loop(2, NY, feed, 0)
    NORM[...] = ACC[...].astype(BF16)
    ring_b.arrive(4)
    share(lambda s: WB.at[others, :, s])
    shared_here(across[-1:])

    o_first = net.number(NY)

    def decode(i, carry):
        k = lax.rem(i + 1, NY)
        keys = jnp.dot(NORM[...], WB[k, 0:4].reshape(E, DLANE), preferred_element_type=F32)
        keys = keys.astype(BF16)
        values = jnp.dot(NORM[...], WB[k, 4:8].reshape(E, DLANE), preferred_element_type=F32)
        values = values.astype(BF16)
        queries = (Q[k].astype(F32) * float(HEAD_DIM) ** -0.5).astype(BF16)
        for pos in range(2):
            for h in range(4):
                cols = slice(h * HEAD_DIM, (h + 1) * HEAD_DIM)
                rows = slice(pos * 256, (pos + 1) * 256)
                toks = slice(pos * SPAN, (pos + 1) * SPAN)
                scores = lax.dot_general(
                    queries[toks, cols], keys[rows, cols], last_last, preferred_element_type=F32
                )
                top = jnp.max(scores, axis=1, keepdims=True)
                parts = jnp.exp(scores - top)
                parts = parts / jnp.sum(parts, axis=1, keepdims=True)
                got = jnp.dot(parts.astype(BF16), values[rows, cols], preferred_element_type=F32)
                OUTB[k, toks, cols] = got.astype(BF16)

        @pl.when(k != 0)
        def _():
            net.describe(OUTB.at[k], ORECV.at[y], o_first + k, (seq, lane(k))).start()

        return carry

    lax.fori_loop(0, NY, decode, 0)
    out_ref[y] = OUTB[0]
    for k in range(1, NY):
        source = lane(NY - k)
        net.recv(o_first + k, ORECV.at[source])
        out_ref[source] = ORECV[source]
    for k in range(1, NY):
        net.describe(OUTB.at[k], OUTB.at[k], o_first + k, partner).wait_send()
    lanes_sent(*kv_numbers, kv_src_two, kv_src_one)
    lanes_sent(*e_numbers, e_src_two, e_src_one)
    for copy in net.sent:
        copy.wait_send()
    assert net.count <= SEMS and net.local_count <= 40


def on_device(
    span_pairs,
    dec_queries,
    database,
    nbr_index,
    nbr_host,
    enc_gain,
    enc_query,
    enc_out,
    ffn_gain,
    ffn_up,
    ffn_down,
    dec_kv,
):
    y = lax.axis_index("mp")
    seq = lax.axis_index("seq")
    db = lax.dynamic_slice_in_dim(database, y * QROWS, QROWS, 1).astype(BF16)
    kv = jnp.moveaxis(span_pairs, 1, 0).reshape(2, CH_DEV, SPAN, LANE)
    wb = jnp.moveaxis(dec_kv, 1, 0).reshape(NZ, NC, 112, DLANE)
    anywhere = pl.BlockSpec(memory_space=pl.ANY)
    in_smem = pl.BlockSpec(memory_space=pltpu.SMEM)
    in_vmem = pl.BlockSpec(memory_space=pltpu.VMEM)
    got = pl.pallas_call(
        kernel,
        out_shape=jax.ShapeDtypeStruct((NY, 128, DLANE), BF16),
        in_specs=[in_smem] * 2 + [anywhere] * 8 + [in_vmem] * 2,
        out_specs=in_vmem,
        scratch_shapes=[
            pltpu.VMEM((NZ, NX, NC, 2, QROWS, E), BF16),
            pltpu.VMEM((NY, NX, NC, 112, LANE), BF16),
            pltpu.VMEM((NY, NX, NC, 32, E), BF16),
            pltpu.VMEM((NY, NX, NC, 112, UNIT), BF16),
            pltpu.VMEM((NY, NX, NC, 64, E), BF16),
            pltpu.VMEM((NY, NZ, NC, 112, DLANE), BF16),
            pltpu.VMEM((NY, 2, 2, SPAN, LANE), BF16),
            pltpu.VMEM((NY, 128, DLANE), BF16),
            pltpu.VMEM((CH_DEV, NEIGH, QROWS, E), BF16),
            pltpu.VMEM((2, NY, NEIGH, QROWS, E), BF16),
            pltpu.VMEM((NY, 128, DLANE), BF16),
            pltpu.VMEM((ROWS, E), BF16),
            pltpu.VMEM((ROWS, E), F32),
            pltpu.VMEM((NY, 128, DLANE), BF16),
            pltpu.SemaphoreType.DMA((SEMS,)),
            pltpu.SemaphoreType.DMA((SEMS,)),
            pltpu.SemaphoreType.DMA((41,)),
        ],
        compiler_params=pltpu.CompilerParams(
            collective_id=0, has_side_effects=True, vmem_limit_bytes=63 * 1024 * 1024
        ),
    )(
        nbr_host,
        nbr_index,
        db,
        kv,
        dec_queries,
        enc_query.reshape(NX, NC, 112, LANE),
        enc_out.reshape(7, 32, E),
        ffn_up.reshape(NX, NC, 112, UNIT),
        ffn_down.reshape(7, 64, E),
        wb,
        enc_gain.reshape(1, E),
        ffn_gain.reshape(1, E),
    )
    got = got.reshape(CH_DEV * SPAN, DLANE).astype(F32)
    token = lax.broadcasted_iota(jnp.int32, got.shape, 0)
    return jnp.where((seq == 0) & (token < SPAN), 0.0, got)


def solution(mesh):
    placed = (
        P("seq", None, "mp"),
        P("seq", "mp"),
        P("seq", None, None),
        P("seq", None),
        P("seq", None),
        P(),
        P(None, "mp"),
        P("mp", None),
        P(),
        P(None, "mp"),
        P("mp", None),
        P(None, None, "mp"),
    )
    return jax.shard_map(
        on_device, mesh=mesh, in_specs=placed, out_specs=P("seq", "mp"), check_vma=False
    )
```

time: 416 us -> 137 us (0.33); the launches traced: 409 us -> 137 us
  waiting for transfers between devices: 167 us -> 0 us
  Pallas kernels: 0 us -> 121 us
  blocking collectives: 93.1 us -> 0 us
  matrix products: 41 us -> 0 us
  local copies, waits for them, and re-layouts: 46.6 us -> 13.1 us
  starting transfers between devices: 33.1 us -> 0 us
  between operations: 13.9 us -> 0.03 us
  other arithmetic: 14.5 us -> 2.69 us
    pallas_call x0 -> x1, Pallas kernels: none -> 121 us  [on_device(): pl.pallas_call(kernel, out_shape=jax.ShapeDtypeStruct((NY, 128, DLANE), B...]
    all_to_all x3 -> x0, waiting for transfers between devices: 121 us -> none  [the longest x1 79.7 us: on_device(): lax.all_to_all(outgoing.reshape(seq_size, slot_cap, SPAN, 2, enc_width),...]
    all_to_all x1 -> x0, blocking collectives: 93.1 us -> none  [on_device(): lax.all_to_all(returning.reshape(seq_size, slot_cap, row_count, width), '...]
    all_gather x3 -> x0, waiting for transfers between devices: 43.4 us -> none  [the longest x1 43.4 us: on_device(): lax.all_gather(used, 'mp', axis=2, tiled=True)]
    dot_general x13 -> x0, matrix products: 41 us -> none  [the longest x1 6.76 us: on_device(): jnp.einsum('mkre,ecd->mkrcd', lax.all_gather(used, 'mp', axis=2, tiled=Tr...]
    all_to_all x3 -> x0, starting transfers between devices: 28.3 us -> none  [the longest x1 13 us: on_device(): lax.all_to_all(out_codes.reshape(seq_size, slot_cap), 'seq', split_axis=0...]
    reshape x5 -> x2, local copies, waits for them, and re-layouts: 17 us -> 2.55 us  [the longest x1 1.28 us: on_device(): enc_gain.reshape(1, E)]
    another operation x4 -> x0, local copies, waits for them, and re-layouts: 10.3 us -> none  [the longest x1 3.97 us: on_device(): dec_pairs[:, :, :, 0].reshape(CH_DEV, NEIGH * NBL, dec_heads, HEAD_DIM)]
  transfers between devices with their start and end apart: 7 -> 0, of which waited for: 4 -> 0; matrix products, arithmetic and copies ran while one was open for 13% -> 0% of each run, Pallas kernels for 0% -> 0%
where the time goes in v1:
time: 137 us
  Pallas kernels  121 us (88%)
  local copies, waits for them, and re-layouts  13.1 us (10%)
  other arithmetic  2.69 us (2%)
    pallas_call x1, Pallas kernels, on_device(): pl.pallas_call(kernel, out_shape=jax.ShapeDtypeStruct((NY, 128, DLANE), B...  121 us
    unnamed x12, local copies, waits for them, and re-layouts  6.33 us

profile of v1, /device:TPU:1, one launch (start us, length us, event | category | flops | bytes accessed | tf_op | source)
XLA Modules:
  0.0 137.0 jit_solution(16886143100515920597)
XLA Ops:
  0.0 0.0 copy-start
  0.0 0.0 copy-start.2
  0.0 0.5 fusion
  0.5 1.3 reshape.33.gain_a
  1.8 1.3 reshape.34.gain_b
  3.1 1.3 copy.18.index_ref
  4.4 1.3 copy.17.host_ref
  5.8 0.0 copy-done
  5.8 0.7 dynamic-slice_convert_fusion.db_hbm
  6.5 0.0 copy-start.1
  6.5 2.1 %copy.14 = bf16[896,224]{1,0:T(8,128)(2,1)} copy(bf16[896,224]{0,1:T(8,128)(2,1)} %param.18) | data formatting | bytes 802816 | tf_op args[6]
  8.6 2.0 %copy.13 = bf16[2,512,224]{2,1,0:T(8,128)(2,1)} copy(bf16[2,512,224]{1,2,0:T(8,128)(2,1)} %bitcast.17) | data formatting | bytes 917504 | tf_op jit(solution)/shard_map/transpose | solution.py:512
  10.6 0.0 copy-done.2
  10.6 1.5 %copy.15 = bf16[896,448]{1,0:T(8,128)(2,1)} copy(bf16[896,448]{0,1:T(8,128)(2,1)S(1)} %copy-done.2) | data formatting | bytes 1605632 | tf_op args[9]
  12.1 0.0 copy-done.1
  12.1 1.6 %copy.16 = bf16[2,896,512]{2,1,0:T(8,128)(2,1)} copy(bf16[2,896,512]{2,0,1:T(2,128)(2,1)S(1)} %bitcast.14) | data formatting | bytes 3670016 | tf_op jit(solution)/shard_map/transpose | solution.py:513
  13.7 0.0 copy-start.3
  13.7 121.2 %shard_map.118 = bf16[4,128,512]{2,1,0:T(8,128)(2,1)} custom-call(s32[8,2]{1,0:T(8,128)} %copy.17.host_ref, s32[8,2]{1,0:T(8,128)} %copy.18.index_ref, bf16[2,32,896]{2,1,0:T(8,128)(2,1)} %dynamic-slice_convert_fusion.db_hbm, bf16[2,8,64,224]{3,2,1,0:T(8,128)(2,1)} %bitcast.13, bf16[512,512]{1,0:T(8,128)(2,1)} %q_hbm.1, bf16[4,2,112,224]{3,2,1,0:T(8,128)(2,1)} %bitcast.15, ...), custom_call_target="tpu_custom_call" | custom-call | tf_op jit(solution)/shard_map/pallas_call | solution.py:517
  134.8 0.0 copy-done.3
  134.8 2.2 %convert_select_fusion = f32[512,512]{1,0:T(8,128)} fusion(bf16[4,128,512]{2,1,0:T(8,128)(2,1)} %shard_map.118, pred[512]{0:T(512)(128)(4,1)S(1)} %copy-done.3), kind=kLoop, calls=%fused_computation | loop fusion | flops 524288 | bytes 1573376 | tf_op jit(solution)/shard_map/jit(_where)/select_n | solution.py:560
Async XLA Ops:
  0.0 5.8 %copy-start = (f32[2,128,896]{2,1,0:T(8,128)S(1)}, f32[2,128,896]{2,1,0:T(8,128)}, u32[]{:S(2)}) copy-start(f32[2,128,896]{2,1,0:T(8,128)} %param.14) | copy-start | bytes 2752516
  0.0 10.6 %copy-start.2 = (bf16[896,448]{0,1:T(8,128)(2,1)S(1)}, bf16[896,448]{0,1:T(8,128)(2,1)}, u32[]{:S(2)}) copy-start(bf16[896,448]{0,1:T(8,128)(2,1)} %param.21) | copy-start | bytes 2408452
  6.5 5.7 %copy-start.1 = (bf16[896,2,512]{2,1,0:T(2,128)(2,1)S(1)}, bf16[896,2,512]{2,1,0:T(2,128)(2,1)}, u32[]{:S(2)}) copy-start(bf16[896,2,512]{2,1,0:T(2,128)(2,1)} %param.23) | copy-start | bytes 5505028
  13.7 121.2 %copy-start.3 = (pred[512]{0:T(512)(128)(4,1)S(1)}, pred[512]{0:T(512)(128)(4,1)}, u32[]{:S(2)}) copy-start(pred[512]{0:T(512)(128)(4,1)} %fusion) | copy-start | bytes 1540
